TPU v7x, 32 devices: a whole 2x2x4 slice. The times are simulated.
32 devices in a mesh: ladder: 4 (over y, x), grp: 8 (over z, core).
Axes of the slice: x: 2, y: 2, z: 4, core: 2. Of those that a mesh axis runs over, the one named last changes fastest.
Arguments:
- init_up: int32 [512, 144], P(('ladder', 'grp')), may hold values 0 or 1
- flip_site: int32 [4, 512], P(None, ('ladder', 'grp')), may hold values from 0 to 143
- accept: int32 [4, 512], P(None, ('ladder', 'grp')), may hold values from 0 to 1
- swap_ok: int32 [4, 2, 128], P(None, None, 'grp'), may hold values 0 or 1
- ladder_bit: int32 [4, 8], P(None, 'grp'), may hold values from 0 to 1
- w_embed: bfloat16 [4, 72], replicated, may hold values from -3 to 3
- pos_embed: float32 [36, 72], replicated, may hold values from -6 to 6
- w_value: bfloat16 [2, 72, 72], replicated, may hold values from -0.75 to 0.75
- mixing: float32 [2, 12, 36, 36], replicated, may hold values from -1 to 1
- w_out: bfloat16 [2, 72, 72], replicated, may hold values from -0.75 to 0.75
- w_in: bfloat16 [2, 72, 288], replicated, may hold values from -0.75 to 0.75
- w_back: bfloat16 [2, 288, 72], replicated, may hold values from -0.375 to 0.375
- w_final: float32 [72, 72], replicated, may hold values from -0.75 to 0.75
- b_final: float32 [72], replicated, may hold values from -5 to 5
Outputs:
- proposal_amp: float32 [4, 512], P(None, ('ladder', 'grp'))
- final_spins: float32 [512, 144], P(('ladder', 'grp'))
- final_amp: float32 [512], P(('ladder', 'grp'))
- accept_counts: float32 [4, 4], P('ladder')
All inputs are finite; a program needn't handle non-finite values. No bound on the sum of `init_up` or of `swap_ok` on one device may be relied on, other than what follows from the above.
Results may differ from a plain program's by a relative error of at most 0.002.
Values sent between devices are 32-bit elements; how exact they have to be, the bound alone decides.
A program may use at most 64 MiB of HBM per device.

v0:
```python
import functools
import math

import jax
import jax.numpy as jnp
from jax import lax
from jax.experimental import pallas as pl
from jax.experimental.pallas import tpu as pltpu
from jax.sharding import PartitionSpec as P

MESH = pl.DeviceIdType.MESH
VMEM = pltpu.VMEM
F32 = jnp.float32
BF16 = jnp.bfloat16


def exchange_kernel(
    rungs, groups, up_ref, flip_ref, accept_ref, ups_ref, flips_ref, accepts_ref, counts_ref,
    send_sem, recv_sem, group_send, group_recv,
):
    rung = lax.axis_index("ladder")
    place = lax.axis_index("grp")
    barrier = pltpu.get_barrier_semaphore()
    for apart in range(1, rungs):
        pl.semaphore_signal(
            barrier, inc=1, device_id=(jnp.bitwise_xor(rung, apart), place), device_id_type=MESH
        )
    for apart in range(1, groups):
        pl.semaphore_signal(
            barrier, inc=1, device_id=(rung, jnp.bitwise_xor(place, apart)), device_id_type=MESH
        )
    pl.semaphore_wait(barrier, rungs - 1 + groups - 1)
    copies = []
    for apart in range(1, rungs):
        target = (jnp.bitwise_xor(rung, apart), place)
        for part, (source, landing) in enumerate(
            ((up_ref, ups_ref), (flip_ref, flips_ref), (accept_ref, accepts_ref))
        ):
            copies.append(
                pltpu.make_async_remote_copy(
                    src_ref=source,
                    dst_ref=landing.at[apart - 1],
                    send_sem=send_sem.at[apart - 1, part],
                    recv_sem=recv_sem.at[apart - 1, part],
                    device_id=target,
                    device_id_type=MESH,
                )
            )
            copies[-1].start()
    for apart in range(1, groups):
        copies.append(
            pltpu.make_async_remote_copy(
                src_ref=accept_ref,
                dst_ref=counts_ref.at[apart - 1],
                send_sem=group_send.at[apart - 1],
                recv_sem=group_recv.at[apart - 1],
                device_id=(rung, jnp.bitwise_xor(place, apart)),
                device_id_type=MESH,
            )
        )
        copies[-1].start()
    for copy in copies:
        copy.wait()


def exchange(init_up, flip_site, accept, rungs, groups):
    return pl.pallas_call(
        functools.partial(exchange_kernel, rungs, groups),
        out_shape=(
            jax.ShapeDtypeStruct((rungs - 1,) + init_up.shape, jnp.int32),
            jax.ShapeDtypeStruct((rungs - 1,) + flip_site.shape, jnp.int32),
            jax.ShapeDtypeStruct((rungs - 1,) + accept.shape, jnp.int32),
            jax.ShapeDtypeStruct((groups - 1,) + accept.shape, jnp.int32),
        ),
        in_specs=[pl.BlockSpec(memory_space=VMEM)] * 3,
        out_specs=[pl.BlockSpec(memory_space=VMEM)] * 4,
        scratch_shapes=[
            pltpu.SemaphoreType.DMA((rungs - 1, 3)),
            pltpu.SemaphoreType.DMA((rungs - 1, 3)),
            pltpu.SemaphoreType.DMA((groups - 1,)),
            pltpu.SemaphoreType.DMA((groups - 1,)),
        ],
        compiler_params=pltpu.CompilerParams(collective_id=0, has_side_effects=True),
        name="exchange",
    )(init_up, flip_site, accept)


def transposed(matrix):
    wide = matrix.shape[1]
    eye = (
        lax.broadcasted_iota(jnp.int32, (wide, wide), 0)
        == lax.broadcasted_iota(jnp.int32, (wide, wide), 1)
    )
    return lax.dot_general(
        eye.astype(F32).astype(matrix.dtype),
        matrix,
        (((1,), (1,)), ((), ())),
        preferred_element_type=F32,
    )


def layer_norm(values):
    scale = 1.0 / values.shape[0]
    center = values - jnp.sum(values, axis=0, keepdims=True) * scale
    spread = jnp.sum(center * center, axis=0, keepdims=True) * scale
    return center * lax.rsqrt(spread + 1e-05)


def gelu(values):
    root = math.sqrt(2.0 / math.pi)
    half = 0.5 * values
    inner = values * (root + (root * 0.044715) * (values * values))
    return half + half * jnp.tanh(inner)


def window_kernel(
    up_ref, flip_ref, accept_ref, ups_ref, flips_ref, accepts_ref, counts_ref,
    swap_ref, bit_ref, w_embed_ref, pos_ref, w_value_ref, mixing_ref, w_out_ref, w_in_ref,
    w_back_ref, w_final_ref, b_final_ref,
    proposal_ref, spins_out_ref, amp_ref, totals_ref,
    event_ref, spin_ref, x_ref, v_ref, embed_ref, wv_ref, wo_ref, wi_ref, wb_ref, pool_ref,
):
    chains, sites = up_ref.shape
    steps = flip_ref.shape[0]
    rungs = ups_ref.shape[0] + 1
    bits = rungs.bit_length() - 1
    patch_count, width = pos_ref.shape
    layers, heads = mixing_ref.shape[:2]
    per_head = width // heads
    hidden_width = w_in_ref.shape[2]
    lanes = event_ref.shape[1]
    side = math.isqrt(sites)
    half_side = side // 2
    rung = lax.axis_index("ladder")

    accepted = accept_ref[...]
    total = accepted + jnp.sum(counts_ref[...], axis=0)
    totals_ref[...] = jnp.sum(total.astype(F32), axis=1, keepdims=True)

    rows = event_ref.shape[0]
    row = lax.broadcasted_iota(jnp.int32, (rows, chains), 0)
    state = [jnp.where(row == 0, apart, -1) for apart in range(rungs)]
    event_ref[...] = jnp.full(event_ref.shape, -1, jnp.int32)
    for step in range(steps):
        mine = slice(step, step + 1)
        moved = []
        for apart in range(rungs):
            sites_here = flip_ref[mine, :] if apart == 0 else flips_ref[apart - 1, mine, :]
            taken = accept_ref[mine, :] if apart == 0 else accepts_ref[apart - 1, mine, :]
            if apart == 0:
                event_ref[:, step * chains : (step + 1) * chains] = jnp.where(
                    row == step + 1, sites_here, state[0]
                )
            moved.append(
                jnp.where(row == step + 1, jnp.where(taken == 1, sites_here, -1), state[apart])
            )
        chosen = bit_ref[mine, :]
        after = []
        for apart in range(rungs):
            here = jnp.bitwise_xor(rung, apart)
            value = moved[apart]
            for bit in range(bits):
                mask = 2**bit
                pair = (here // (2 * mask)) * mask + lax.rem(here, mask)
                decided = jnp.where(chosen == bit, swap_ref[step, pl.ds(pair, 1), :], 0)
                value = jnp.where(
                    jnp.broadcast_to(decided, value.shape) == 1, moved[apart ^ mask], value
                )
            after.append(value)
        state = after
    event_ref[:, steps * chains : (steps + 1) * chains] = state[0]

    events = event_ref[...]
    lane = lax.broadcasted_iota(jnp.int32, (1, lanes), 1)
    wanted = events[0:1, :] * chains + lax.rem(lane, chains)
    member = lax.broadcasted_iota(jnp.int32, (rungs * chains, lanes), 0)
    pick = (member == wanted).astype(F32).astype(BF16)
    everyone = jnp.concatenate(
        [up_ref[...], ups_ref[...].reshape((rungs - 1) * chains, sites)], axis=0
    )
    picked = lax.dot_general(
        everyone.astype(F32).astype(BF16), pick, (((0,), (0,)), ((), ())),
        preferred_element_type=F32,
    )
    spins = 2.0 * picked - 1.0
    site = lax.broadcasted_iota(jnp.int32, (sites, lanes), 0)
    for step in range(steps):
        spins = jnp.where(site == events[step + 1 : step + 2, :], -spins, spins)
    spin_ref[...] = spins
    last = (
        lax.broadcasted_iota(jnp.int32, (chains, lanes), 1)
        == lax.broadcasted_iota(jnp.int32, (chains, lanes), 0) + steps * chains
    )
    spins_out_ref[...] = lax.dot_general(
        last.astype(F32).astype(BF16), spins.astype(BF16), (((1,), (1,)), ((), ())),
        preferred_element_type=F32,
    )

    depth = embed_ref.shape[1]
    part_rows = (depth - 8) // 3
    pos = pos_ref[...]
    high = pos.astype(BF16)
    middle = (pos - high.astype(F32)).astype(BF16)
    low = (pos - high.astype(F32) - middle.astype(F32)).astype(BF16)
    blank = jnp.zeros((part_rows - patch_count, width), F32)
    pieces = [w_embed_ref[...].astype(F32), jnp.zeros((8 - w_embed_ref.shape[0], width), F32)]
    for part in (high, middle, low):
        pieces += [part.astype(F32), blank]
    embed_ref[...] = transposed(jnp.concatenate(pieces, axis=0).astype(BF16)).astype(BF16)
    for layer in range(layers):
        wv_ref[layer] = transposed(w_value_ref[layer]).astype(BF16)
        wo_ref[layer] = transposed(w_out_ref[layer]).astype(BF16)
        wi_ref[layer] = transposed(w_in_ref[layer]).astype(BF16)
        wb_ref[layer] = transposed(w_back_ref[layer]).astype(BF16)

    def rows_of(patch):
        return pl.ds(pl.multiple_of(patch * width, 8), width)

    def pair_of(ref, first):
        return jnp.concatenate([ref[rows_of(first), :], ref[rows_of(first + 1), :]], axis=1)

    def put_pair(ref, first, value):
        ref[rows_of(first), :] = value[:, :lanes]
        ref[rows_of(first + 1), :] = value[:, lanes:]

    def matmul(left, right):
        return jnp.dot(left, right, preferred_element_type=F32)

    slot = lax.broadcasted_iota(jnp.int32, (depth, lanes), 0)
    spot = jnp.where(slot < 8, -1, lax.rem(slot + (part_rows - 8), part_rows))
    eight = lax.broadcasted_iota(jnp.int32, (8, lanes), 0)

    def embed_input(patch):
        top = (patch // half_side) * (2 * side) + lax.rem(patch, half_side) * 2
        block = jnp.zeros((8, lanes), F32)
        for index, offset in enumerate((0, 1, side, side + 1)):
            block = jnp.where(eight == index, spin_ref[pl.ds(top + offset, 1), :], block)
        onehot = (spot == patch).astype(F32)
        return jnp.concatenate([block, onehot[8:]], axis=0).astype(BF16)

    def start(pair, carry):
        first = pair * 2
        right = jnp.concatenate([embed_input(first), embed_input(first + 1)], axis=1)
        stream = matmul(embed_ref[...], right)
        put_pair(x_ref, first, stream)
        put_pair(v_ref, first, matmul(wv_ref[0], layer_norm(stream).astype(BF16)))
        return carry

    lax.fori_loop(0, patch_count // 2, start, 0)
    pool_ref[...] = jnp.zeros(pool_ref.shape, F32)

    for layer in range(layers):
        for head in range(heads):
            places = [
                pl.ds(head * per_head + index, patch_count, stride=width)
                for index in range(per_head)
            ]
            value = jnp.concatenate([v_ref[spot_rows, :] for spot_rows in places], axis=1)
            mixed = matmul(mixing_ref[layer, head].astype(BF16), value.astype(BF16))
            for index, spot_rows in enumerate(places):
                v_ref[spot_rows, :] = mixed[:, index * lanes : (index + 1) * lanes]

        def block(pair, carry, layer=layer):
            first = pair * 2
            stream = pair_of(x_ref, first) + matmul(
                wo_ref[layer], pair_of(v_ref, first).astype(BF16)
            )
            normed = layer_norm(stream).astype(BF16)
            hidden = gelu(matmul(wi_ref[layer], normed)).astype(BF16)
            stream = stream + matmul(wb_ref[layer], hidden)
            normed = layer_norm(stream)
            if layer + 1 < layers:
                put_pair(x_ref, first, stream)
                put_pair(v_ref, first, matmul(wv_ref[layer + 1], normed.astype(BF16)))
            else:
                pool_ref[...] += normed[:, :lanes] + normed[:, lanes:]
            return carry

        lax.fori_loop(0, patch_count // 2, block, 0)

    pooled = pool_ref[...] / half_side
    bias = jnp.transpose(jnp.broadcast_to(b_final_ref[...], (lanes, width)))
    final = lax.dot_general(
        w_final_ref[...], pooled, (((0,), (0,)), ((), ())),
        preferred_element_type=F32, precision=lax.Precision.HIGHEST,
    ) + bias
    size = jnp.abs(final)
    curve = size + jnp.log1p(jnp.exp(-2.0 * size)) - math.log(2.0)
    amps = jnp.sum(curve, axis=0, keepdims=True) * (1.0 / width)
    for step in range(steps):
        proposal_ref[step : step + 1, :] = amps[:, step * chains : (step + 1) * chains]
    amp_ref[...] = amps[:, steps * chains : (steps + 1) * chains]


def on_device(
    init_up, flip_site, accept, swap_ok, ladder_bit, w_embed, pos_embed, w_value, mixing, w_out,
    w_in, w_back, w_final, b_final,
):
    rungs, groups = lax.axis_size("ladder"), lax.axis_size("grp")
    chains, sites = init_up.shape
    steps = flip_site.shape[0]
    patch_count, width = pos_embed.shape
    layers, hidden_width = w_in.shape[0], w_in.shape[2]
    ups, flips, accepts, counts = exchange(init_up, flip_site, accept, rungs, groups)
    lanes = -(-(steps + 1) * chains // 128) * 128
    rows = -(-(steps + 1) // 8) * 8
    depth = 8 + 3 * (-(-patch_count // 8) * 8)
    proposals, spins, amp, totals = pl.pallas_call(
        window_kernel,
        out_shape=(
            jax.ShapeDtypeStruct((steps, chains), F32),
            jax.ShapeDtypeStruct((chains, sites), F32),
            jax.ShapeDtypeStruct((1, chains), F32),
            jax.ShapeDtypeStruct((steps, 1), F32),
        ),
        in_specs=[pl.BlockSpec(memory_space=VMEM)] * 18,
        out_specs=[pl.BlockSpec(memory_space=VMEM)] * 4,
        scratch_shapes=[
            VMEM((rows, lanes), jnp.int32),
            VMEM((sites, lanes), F32),
            VMEM((patch_count * width, lanes), F32),
            VMEM((patch_count * width, lanes), F32),
            VMEM((width, depth), BF16),
            VMEM((layers, width, width), BF16),
            VMEM((layers, width, width), BF16),
            VMEM((layers, hidden_width, width), BF16),
            VMEM((layers, width, hidden_width), BF16),
            VMEM((width, lanes), F32),
        ],
        name="window",
    )(
        init_up, flip_site, accept, ups, flips, accepts, counts, swap_ok, ladder_bit, w_embed,
        pos_embed, w_value, mixing, w_out, w_in, w_back, w_final, b_final.reshape(1, width),
    )
    return proposals, spins, amp.reshape(chains), totals.reshape(1, steps)


def solution(mesh):
    placed = (
        P(("ladder", "grp"), None),
        P(None, ("ladder", "grp")),
        P(None, ("ladder", "grp")),
        P(None, None, "grp"),
        P(None, "grp"),
    ) + (P(),) * 9
    return jax.shard_map(
        on_device,
        mesh=mesh,
        in_specs=placed,
        out_specs=(
            P(None, ("ladder", "grp")),
            P(("ladder", "grp"), None),
            P(("ladder", "grp")),
            P("ladder", None),
        ),
        check_vma=False,
    )
```

profile of v0, /device:TPU:0, one launch (start us, length us, event | category | flops | bytes accessed | tf_op | source)
XLA Modules:
  0.0 51.6 jit_solution(15083166238530769578)
XLA Ops:
  0.6 0.0 copy-start.1
  0.6 0.6 %copy-done.1 = s32[4,1]{0,1:T(1,128)S(1)} copy-done((s32[4,1]{0,1:T(1,128)S(1)}, s32[4,1]{0,1:T(1,128)}, u32[]{:S(2)}) %copy-start.1) | copy-done | bytes 40
  1.3 0.7 %copy.21.bit_ref = s32[4,1]{1,0:T(4,128)} copy(s32[4,1]{0,1:T(1,128)S(1)} %copy-done.1) | data formatting | bytes 32 | tf_op args[4]
  2.0 11.2 %exchange.1 = (s32[3,16,144]{2,1,0:T(8,128)}, s32[3,4,16]{2,1,0:T(4,128)}, s32[3,4,16]{2,1,0:T(4,128)}, s32[7,4,16]{2,1,0:T(4,128)}) custom-call(s32[16,144]{1,0:T(8,128)} %up_ref.3, s32[4,16]{1,0:T(4,128)} %flip_ref.3, s32[4,16]{1,0:T(4,128)} %accept_ref.3), custom_call_target="tpu_custom_call" | custom-call | tf_op jit(solution)/shard_map/exchange/pallas_call | solution.py:67
  13.1 1.7 %copy.23.w_back_ref = bf16[2,288,72]{2,1,0:T(8,128)(2,1)} copy(bf16[2,288,72]{1,2,0:T(8,128)(2,1)} %param.25) | data formatting | bytes 165888 | tf_op args[11]
  14.8 1.8 %copy.22.mixing_ref = f32[2,12,36,36]{3,2,1,0:T(8,128)} copy(f32[2,12,36,36]{3,0,2,1:T(2,128)} %param.22) | data formatting | bytes 248832 | tf_op args[8]
  16.7 33.6 %window.1 = (f32[4,16]{1,0:T(4,128)}, f32[16,144]{1,0:T(8,128)}, f32[1,16]{1,0:T(1,128)}, f32[4,1]{1,0:T(4,128)}) custom-call(s32[16,144]{1,0:T(8,128)} %up_ref.3, s32[4,16]{1,0:T(4,128)} %flip_ref.3, s32[4,16]{1,0:T(4,128)} %accept_ref.3, s32[3,16,144]{2,1,0:T(8,128)} %get-tuple-element.12.ups_ref, s32[3,4,16]{2,1,0:T(4,128)} %get-tuple-element.13.flips_ref, ...), custom_call_target="tpu_custom_call" | custom-call | tf_op jit(solution)/shard_map/window/pallas_call | solution.py:308
  50.3 0.0 copy-start
  50.3 0.7 %copy-done = f32[4,1]{1,0:T(4,128)S(1)} copy-done((f32[4,1]{1,0:T(4,128)S(1)}, f32[4,1]{1,0:T(4,128)}, u32[]{:S(2)}) %copy-start) | copy-done | bytes 40
  50.9 0.6 %reduce = f32[4]{0:T(128)} reduce(f32[4,1]{1,0:T(4,128)S(1)} %copy-done, f32[]{:T(128)} %constant.4), dimensions={1}, to_apply=%get-tuple-element.19.reduce_sub_computation | reduce | bytes 36 | tf_op jit(solution)/shard_map/window/pallas_call | solution.py:308
Async XLA Ops:
  0.6 0.7 %copy-start.1 = (s32[4,1]{0,1:T(1,128)S(1)}, s32[4,1]{0,1:T(1,128)}, u32[]{:S(2)}) copy-start(s32[4,1]{0,1:T(1,128)} %param.18) | copy-start | bytes 52
  50.3 0.7 %copy-start = (f32[4,1]{1,0:T(4,128)S(1)}, f32[4,1]{1,0:T(4,128)}, u32[]{:S(2)}) copy-start(f32[4,1]{1,0:T(4,128)} %get-tuple-element.19) | copy-start | bytes 52
where the time goes:
time: 51.9 us; the launch traced here: 51.6 us
  Pallas kernels  44.8 us (86%)
  local copies, waits for them, and re-layouts  5.53 us (11%)
  between operations  0.66 us (1%)
  other arithmetic  0.63 us (1%)
    pallas_call x1, Pallas kernels, on_device(): pl.pallas_call(window_kernel, out_shape=(jax.ShapeDtypeStruct((steps, cha...  33.6 us
    pallas_call x1, Pallas kernels, exchange(): pl.pallas_call(functools.partial(exchange_kernel, rungs, groups), out_sha...  11.2 us
    unnamed x7, local copies, waits for them, and re-layouts  5.53 us

commit v1 on v0

--- a/solution.py
+++ b/solution.py
@@ -12,6 +12,7 @@
 VMEM = pltpu.VMEM
 F32 = jnp.float32
 BF16 = jnp.bfloat16
+GROUP = 9
 
 
 def exchange_kernel(
@@ -106,11 +107,10 @@
     return center * lax.rsqrt(spread + 1e-05)
 
 
-def gelu(values):
+def twice_gelu(values):
     root = math.sqrt(2.0 / math.pi)
-    half = 0.5 * values
     inner = values * (root + (root * 0.044715) * (values * values))
-    return half + half * jnp.tanh(inner)
+    return values + values * jnp.tanh(inner)
 
 
 def window_kernel(
@@ -125,7 +125,8 @@
     rungs = ups_ref.shape[0] + 1
     bits = rungs.bit_length() - 1
     patch_count, width = pos_ref.shape
-    layers, heads = mixing_ref.shape[:2]
+    layers = w_value_ref.shape[0]
+    heads = mixing_ref.shape[0] // (layers * patch_count)
     per_head = width // heads
     hidden_width = w_in_ref.shape[2]
     lanes = event_ref.shape[1]
@@ -135,7 +136,10 @@
 
     accepted = accept_ref[...]
     total = accepted + jnp.sum(counts_ref[...], axis=0)
-    totals_ref[...] = jnp.sum(total.astype(F32), axis=1, keepdims=True)
+    totals_ref[...] = lax.dot_general(
+        jnp.ones((1, chains), F32), total.astype(F32), (((1,), (1,)), ((), ())),
+        preferred_element_type=F32, precision=lax.Precision.HIGHEST,
+    )
 
     rows = event_ref.shape[0]
     row = lax.broadcasted_iota(jnp.int32, (rows, chains), 0)
@@ -154,7 +158,7 @@
             moved.append(
                 jnp.where(row == step + 1, jnp.where(taken == 1, sites_here, -1), state[apart])
             )
-        chosen = bit_ref[mine, :]
+        chosen = bit_ref[:, mine]
         after = []
         for apart in range(rungs):
             here = jnp.bitwise_xor(rung, apart)
@@ -211,7 +215,7 @@
         wv_ref[layer] = transposed(w_value_ref[layer]).astype(BF16)
         wo_ref[layer] = transposed(w_out_ref[layer]).astype(BF16)
         wi_ref[layer] = transposed(w_in_ref[layer]).astype(BF16)
-        wb_ref[layer] = transposed(w_back_ref[layer]).astype(BF16)
+        wb_ref[layer] = (w_back_ref[layer].astype(F32) * 0.5).astype(BF16)
 
     def rows_of(patch):
         return pl.ds(pl.multiple_of(patch * width, 8), width)
@@ -238,15 +242,20 @@
         onehot = (spot == patch).astype(F32)
         return jnp.concatenate([block, onehot[8:]], axis=0).astype(BF16)
 
-    def start(pair, carry):
-        first = pair * 2
-        right = jnp.concatenate([embed_input(first), embed_input(first + 1)], axis=1)
-        stream = matmul(embed_ref[...], right)
-        put_pair(x_ref, first, stream)
-        put_pair(v_ref, first, matmul(wv_ref[0], layer_norm(stream).astype(BF16)))
+    def start(index, carry):
+        firsts = [(index * GROUP + member) * 2 for member in range(GROUP)]
+        streams = []
+        for first in firsts:
+            right = jnp.concatenate([embed_input(first), embed_input(first + 1)], axis=1)
+            streams.append(matmul(embed_ref[...], right))
+        norms = [layer_norm(stream).astype(BF16) for stream in streams]
+        values = [matmul(wv_ref[0], norm) for norm in norms]
+        for first, stream, value in zip(firsts, streams, values):
+            put_pair(x_ref, first, stream)
+            put_pair(v_ref, first, value)
         return carry
 
-    lax.fori_loop(0, patch_count // 2, start, 0)
+    lax.fori_loop(0, patch_count // (2 * GROUP), start, 0)
     pool_ref[...] = jnp.zeros(pool_ref.shape, F32)
 
     for layer in range(layers):
@@ -256,27 +265,38 @@
                 for index in range(per_head)
             ]
             value = jnp.concatenate([v_ref[spot_rows, :] for spot_rows in places], axis=1)
-            mixed = matmul(mixing_ref[layer, head].astype(BF16), value.astype(BF16))
+            across = mixing_ref[
+                pl.ds(head * patch_count * layers + layer, patch_count, stride=layers), :
+            ]
+            mixed = matmul(across.astype(BF16), value.astype(BF16))
             for index, spot_rows in enumerate(places):
                 v_ref[spot_rows, :] = mixed[:, index * lanes : (index + 1) * lanes]
 
-        def block(pair, carry, layer=layer):
-            first = pair * 2
-            stream = pair_of(x_ref, first) + matmul(
-                wo_ref[layer], pair_of(v_ref, first).astype(BF16)
-            )
-            normed = layer_norm(stream).astype(BF16)
-            hidden = gelu(matmul(wi_ref[layer], normed)).astype(BF16)
-            stream = stream + matmul(wb_ref[layer], hidden)
-            normed = layer_norm(stream)
+        def block(index, carry, layer=layer):
+            firsts = [(index * GROUP + member) * 2 for member in range(GROUP)]
+            olds = [pair_of(x_ref, first) for first in firsts]
+            mixes = [pair_of(v_ref, first).astype(BF16) for first in firsts]
+            streams = [old + matmul(wo_ref[layer], mix) for old, mix in zip(olds, mixes)]
+            norms = [layer_norm(stream).astype(BF16) for stream in streams]
+            hiddens = [
+                twice_gelu(matmul(wi_ref[layer], norm)).astype(BF16) for norm in norms
+            ]
+            streams = [
+                stream + matmul(wb_ref[layer], hidden)
+                for stream, hidden in zip(streams, hiddens)
+            ]
+            norms = [layer_norm(stream) for stream in streams]
             if layer + 1 < layers:
-                put_pair(x_ref, first, stream)
-                put_pair(v_ref, first, matmul(wv_ref[layer + 1], normed.astype(BF16)))
+                values = [matmul(wv_ref[layer + 1], norm.astype(BF16)) for norm in norms]
+                for first, stream, value in zip(firsts, streams, values):
+                    put_pair(x_ref, first, stream)
+                    put_pair(v_ref, first, value)
             else:
-                pool_ref[...] += normed[:, :lanes] + normed[:, lanes:]
+                parts = [norm[:, :lanes] + norm[:, lanes:] for norm in norms]
+                pool_ref[...] += functools.reduce(jnp.add, parts)
             return carry
 
-        lax.fori_loop(0, patch_count // 2, block, 0)
+        lax.fori_loop(0, patch_count // (2 * GROUP), block, 0)
 
     pooled = pool_ref[...] / half_side
     bias = jnp.transpose(jnp.broadcast_to(b_final_ref[...], (lanes, width)))
@@ -311,7 +331,7 @@
             jax.ShapeDtypeStruct((steps, chains), F32),
             jax.ShapeDtypeStruct((chains, sites), F32),
             jax.ShapeDtypeStruct((1, chains), F32),
-            jax.ShapeDtypeStruct((steps, 1), F32),
+            jax.ShapeDtypeStruct((1, steps), F32),
         ),
         in_specs=[pl.BlockSpec(memory_space=VMEM)] * 18,
         out_specs=[pl.BlockSpec(memory_space=VMEM)] * 4,
@@ -329,10 +349,11 @@
         ],
         name="window",
     )(
-        init_up, flip_site, accept, ups, flips, accepts, counts, swap_ok, ladder_bit, w_embed,
-        pos_embed, w_value, mixing, w_out, w_in, w_back, w_final, b_final.reshape(1, width),
-    )
-    return proposals, spins, amp.reshape(chains), totals.reshape(1, steps)
+        init_up, flip_site, accept, ups, flips, accepts, counts, swap_ok, ladder_bit.T, w_embed,
+        pos_embed, w_value, mixing.transpose(1, 2, 0, 3).reshape(-1, patch_count), w_out, w_in,
+        w_back.swapaxes(1, 2), w_final, b_final.reshape(1, width),
+    )
+    return proposals, spins, amp.reshape(chains), totals
 
 
 def solution(mesh):

time: 51.9 us -> 22.7 us (0.44)
  Pallas kernels: 44.8 us -> 21.8 us
  local copies, waits for them, and re-layouts: 5.53 us -> 0 us
  other arithmetic: 0.63 us -> 0 us
    pallas_call x1, Pallas kernels: 33.6 us -> 10.6 us  [on_device(): pl.pallas_call(window_kernel, out_shape=(jax.ShapeDtypeStruct((steps, cha...]
    unnamed x7 -> x0, local copies, waits for them, and re-layouts: 5.53 us -> none
    pallas_call x1 -> x0, other arithmetic: 0.63 us -> none  [on_device(): pl.pallas_call(window_kernel, out_shape=(jax.ShapeDtypeStruct((steps, cha...]
where the time goes in v1:
time: 22.7 us; the launch traced here: 22.5 us
  Pallas kernels  21.8 us (96%)
  between operations  0.64 us (3%)
    pallas_call x1, Pallas kernels, exchange(): pl.pallas_call(functools.partial(exchange_kernel, rungs, groups), out_sha...  11.2 us
    pallas_call x1, Pallas kernels, on_device(): pl.pallas_call(window_kernel, out_shape=(jax.ShapeDtypeStruct((steps, cha...  10.6 us

profile of v1, /device:TPU:0, one launch (start us, length us, event | category | flops | bytes accessed | tf_op | source)
XLA Modules:
  0.0 22.5 jit_solution(17887470865317587007)
XLA Ops:
  0.6 11.2 %exchange.1 = (s32[3,16,144]{2,1,0:T(8,128)}, s32[3,4,16]{2,1,0:T(4,128)}, s32[3,4,16]{2,1,0:T(4,128)}, s32[7,4,16]{2,1,0:T(4,128)}) custom-call(s32[16,144]{1,0:T(8,128)} %up_ref.3, s32[4,16]{1,0:T(4,128)} %flip_ref.3, s32[4,16]{1,0:T(4,128)} %accept_ref.3), custom_call_target="tpu_custom_call" | custom-call | tf_op jit(solution)/shard_map/exchange/pallas_call | solution.py:68
  11.8 10.6 %window.1 = (f32[4,16]{1,0:T(4,128)}, f32[16,144]{1,0:T(8,128)}, f32[1,16]{1,0:T(1,128)}, f32[1,4]{1,0:T(1,128)}) custom-call(s32[16,144]{1,0:T(8,128)} %up_ref.3, s32[4,16]{1,0:T(4,128)} %flip_ref.3, s32[4,16]{1,0:T(4,128)} %accept_ref.3, s32[3,16,144]{2,1,0:T(8,128)} %get-tuple-element.12.ups_ref, s32[3,4,16]{2,1,0:T(4,128)} %get-tuple-element.13.flips_ref, ...), custom_call_target="tpu_custom_call" | custom-call | tf_op jit(solution)/shard_map/window/pallas_call | solution.py:328

commit v2 on v1

--- a/solution.py
+++ b/solution.py
@@ -15,77 +15,6 @@
 GROUP = 9
 
 
-def exchange_kernel(
-    rungs, groups, up_ref, flip_ref, accept_ref, ups_ref, flips_ref, accepts_ref, counts_ref,
-    send_sem, recv_sem, group_send, group_recv,
-):
-    rung = lax.axis_index("ladder")
-    place = lax.axis_index("grp")
-    barrier = pltpu.get_barrier_semaphore()
-    for apart in range(1, rungs):
-        pl.semaphore_signal(
-            barrier, inc=1, device_id=(jnp.bitwise_xor(rung, apart), place), device_id_type=MESH
-        )
-    for apart in range(1, groups):
-        pl.semaphore_signal(
-            barrier, inc=1, device_id=(rung, jnp.bitwise_xor(place, apart)), device_id_type=MESH
-        )
-    pl.semaphore_wait(barrier, rungs - 1 + groups - 1)
-    copies = []
-    for apart in range(1, rungs):
-        target = (jnp.bitwise_xor(rung, apart), place)
-        for part, (source, landing) in enumerate(
-            ((up_ref, ups_ref), (flip_ref, flips_ref), (accept_ref, accepts_ref))
-        ):
-            copies.append(
-                pltpu.make_async_remote_copy(
-                    src_ref=source,
-                    dst_ref=landing.at[apart - 1],
-                    send_sem=send_sem.at[apart - 1, part],
-                    recv_sem=recv_sem.at[apart - 1, part],
-                    device_id=target,
-                    device_id_type=MESH,
-                )
-            )
-            copies[-1].start()
-    for apart in range(1, groups):
-        copies.append(
-            pltpu.make_async_remote_copy(
-                src_ref=accept_ref,
-                dst_ref=counts_ref.at[apart - 1],
-                send_sem=group_send.at[apart - 1],
-                recv_sem=group_recv.at[apart - 1],
-                device_id=(rung, jnp.bitwise_xor(place, apart)),
-                device_id_type=MESH,
-            )
-        )
-        copies[-1].start()
-    for copy in copies:
-        copy.wait()
-
-
-def exchange(init_up, flip_site, accept, rungs, groups):
-    return pl.pallas_call(
-        functools.partial(exchange_kernel, rungs, groups),
-        out_shape=(
-            jax.ShapeDtypeStruct((rungs - 1,) + init_up.shape, jnp.int32),
-            jax.ShapeDtypeStruct((rungs - 1,) + flip_site.shape, jnp.int32),
-            jax.ShapeDtypeStruct((rungs - 1,) + accept.shape, jnp.int32),
-            jax.ShapeDtypeStruct((groups - 1,) + accept.shape, jnp.int32),
-        ),
-        in_specs=[pl.BlockSpec(memory_space=VMEM)] * 3,
-        out_specs=[pl.BlockSpec(memory_space=VMEM)] * 4,
-        scratch_shapes=[
-            pltpu.SemaphoreType.DMA((rungs - 1, 3)),
-            pltpu.SemaphoreType.DMA((rungs - 1, 3)),
-            pltpu.SemaphoreType.DMA((groups - 1,)),
-            pltpu.SemaphoreType.DMA((groups - 1,)),
-        ],
-        compiler_params=pltpu.CompilerParams(collective_id=0, has_side_effects=True),
-        name="exchange",
-    )(init_up, flip_site, accept)
-
-
 def transposed(matrix):
     wide = matrix.shape[1]
     eye = (
@@ -114,15 +43,14 @@
 
 
 def window_kernel(
-    up_ref, flip_ref, accept_ref, ups_ref, flips_ref, accepts_ref, counts_ref,
-    swap_ref, bit_ref, w_embed_ref, pos_ref, w_value_ref, mixing_ref, w_out_ref, w_in_ref,
-    w_back_ref, w_final_ref, b_final_ref,
-    proposal_ref, spins_out_ref, amp_ref, totals_ref,
-    event_ref, spin_ref, x_ref, v_ref, embed_ref, wv_ref, wo_ref, wi_ref, wb_ref, pool_ref,
+    rungs, groups, up_ref, flip_ref, accept_ref, swap_ref, bit_ref, w_embed_ref, pos_ref, w_value_ref, mixing_ref, w_out_ref, w_in_ref,
+    w_back_ref,
+    pool_ref, spins_out_ref, totals_ref,
+    event_ref, spin_ref, x_ref, v_ref, embed_ref, wv_ref, wo_ref, wi_ref, wb_ref,
+    ups_ref, flips_ref, accepts_ref, counts_ref, send_sem, recv_sem, group_send, group_recv,
 ):
     chains, sites = up_ref.shape
     steps = flip_ref.shape[0]
-    rungs = ups_ref.shape[0] + 1
     bits = rungs.bit_length() - 1
     patch_count, width = pos_ref.shape
     layers = w_value_ref.shape[0]
@@ -134,12 +62,60 @@
     half_side = side // 2
     rung = lax.axis_index("ladder")
 
-    accepted = accept_ref[...]
-    total = accepted + jnp.sum(counts_ref[...], axis=0)
-    totals_ref[...] = lax.dot_general(
-        jnp.ones((1, chains), F32), total.astype(F32), (((1,), (1,)), ((), ())),
-        preferred_element_type=F32, precision=lax.Precision.HIGHEST,
-    )
+    place = lax.axis_index("grp")
+    over_ladder = [(jnp.bitwise_xor(rung, apart), place) for apart in range(1, rungs)]
+    over_group = [(rung, jnp.bitwise_xor(place, apart)) for apart in range(1, groups)]
+    barrier = pltpu.get_barrier_semaphore()
+    for device in over_ladder + over_group:
+        pl.semaphore_signal(barrier, inc=1, device_id=device, device_id_type=MESH)
+    pl.semaphore_wait(barrier, rungs - 1 + groups - 1)
+    walkers = [
+        pltpu.make_async_remote_copy(
+            src_ref=source,
+            dst_ref=landing.at[index],
+            send_sem=send_sem.at[index, part],
+            recv_sem=recv_sem.at[index, part],
+            device_id=device,
+            device_id_type=MESH,
+        )
+        for index, device in enumerate(over_ladder)
+        for part, (source, landing) in enumerate(
+            ((up_ref, ups_ref), (flip_ref, flips_ref), (accept_ref, accepts_ref))
+        )
+    ]
+    tallies = [
+        pltpu.make_async_remote_copy(
+            src_ref=accept_ref,
+            dst_ref=counts_ref.at[index],
+            send_sem=group_send.at[index],
+            recv_sem=group_recv.at[index],
+            device_id=device,
+            device_id_type=MESH,
+        )
+        for index, device in enumerate(over_group)
+    ]
+    for copy in walkers + tallies:
+        copy.start()
+
+    depth = embed_ref.shape[1]
+    part_rows = (depth - 8) // 3
+    pos = pos_ref[...]
+    high = pos.astype(BF16)
+    middle = (pos - high.astype(F32)).astype(BF16)
+    low = (pos - high.astype(F32) - middle.astype(F32)).astype(BF16)
+    blank = jnp.zeros((part_rows - patch_count, width), F32)
+    pieces = [w_embed_ref[...].astype(F32), jnp.zeros((8 - w_embed_ref.shape[0], width), F32)]
+    for part in (high, middle, low):
+        pieces += [part.astype(F32), blank]
+    embed_ref[...] = transposed(jnp.concatenate(pieces, axis=0).astype(BF16)).astype(BF16)
+    for layer in range(layers):
+        wv_ref[layer] = transposed(w_value_ref[layer]).astype(BF16)
+        wo_ref[layer] = transposed(w_out_ref[layer]).astype(BF16)
+        wi_ref[layer] = transposed(w_in_ref[layer]).astype(BF16)
+        wb_ref[layer] = (w_back_ref[layer].astype(F32) * 0.5).astype(BF16)
+
+    for copy in walkers:
+        copy.wait()
 
     rows = event_ref.shape[0]
     row = lax.broadcasted_iota(jnp.int32, (rows, chains), 0)
@@ -200,23 +176,6 @@
         preferred_element_type=F32,
     )
 
-    depth = embed_ref.shape[1]
-    part_rows = (depth - 8) // 3
-    pos = pos_ref[...]
-    high = pos.astype(BF16)
-    middle = (pos - high.astype(F32)).astype(BF16)
-    low = (pos - high.astype(F32) - middle.astype(F32)).astype(BF16)
-    blank = jnp.zeros((part_rows - patch_count, width), F32)
-    pieces = [w_embed_ref[...].astype(F32), jnp.zeros((8 - w_embed_ref.shape[0], width), F32)]
-    for part in (high, middle, low):
-        pieces += [part.astype(F32), blank]
-    embed_ref[...] = transposed(jnp.concatenate(pieces, axis=0).astype(BF16)).astype(BF16)
-    for layer in range(layers):
-        wv_ref[layer] = transposed(w_value_ref[layer]).astype(BF16)
-        wo_ref[layer] = transposed(w_out_ref[layer]).astype(BF16)
-        wi_ref[layer] = transposed(w_in_ref[layer]).astype(BF16)
-        wb_ref[layer] = (w_back_ref[layer].astype(F32) * 0.5).astype(BF16)
-
     def rows_of(patch):
         return pl.ds(pl.multiple_of(patch * width, 8), width)
 
@@ -298,6 +257,23 @@
 
         lax.fori_loop(0, patch_count // (2 * GROUP), block, 0)
 
+    for copy in tallies:
+        copy.wait()
+    accepted = accept_ref[...] + jnp.sum(counts_ref[...], axis=0)
+    totals_ref[...] = lax.dot_general(
+        jnp.ones((1, chains), F32), accepted.astype(F32), (((1,), (1,)), ((), ())),
+        preferred_element_type=F32, precision=lax.Precision.HIGHEST,
+    )
+
+
+def head_kernel(
+    half_side, pool_ref, spins_ref, totals_ref, w_final_ref, b_final_ref,
+    proposal_ref, spins_out_ref, amp_ref, totals_out_ref,
+):
+    width, lanes = pool_ref.shape
+    steps, chains = proposal_ref.shape
+    spins_out_ref[...] = spins_ref[...]
+    totals_out_ref[...] = totals_ref[...]
     pooled = pool_ref[...] / half_side
     bias = jnp.transpose(jnp.broadcast_to(b_final_ref[...], (lanes, width)))
     final = lax.dot_general(
@@ -321,20 +297,18 @@
     steps = flip_site.shape[0]
     patch_count, width = pos_embed.shape
     layers, hidden_width = w_in.shape[0], w_in.shape[2]
-    ups, flips, accepts, counts = exchange(init_up, flip_site, accept, rungs, groups)
     lanes = -(-(steps + 1) * chains // 128) * 128
     rows = -(-(steps + 1) // 8) * 8
     depth = 8 + 3 * (-(-patch_count // 8) * 8)
-    proposals, spins, amp, totals = pl.pallas_call(
-        window_kernel,
+    pool, spins, totals = pl.pallas_call(
+        functools.partial(window_kernel, rungs, groups),
         out_shape=(
-            jax.ShapeDtypeStruct((steps, chains), F32),
+            jax.ShapeDtypeStruct((width, lanes), F32),
             jax.ShapeDtypeStruct((chains, sites), F32),
-            jax.ShapeDtypeStruct((1, chains), F32),
             jax.ShapeDtypeStruct((1, steps), F32),
         ),
-        in_specs=[pl.BlockSpec(memory_space=VMEM)] * 18,
-        out_specs=[pl.BlockSpec(memory_space=VMEM)] * 4,
+        in_specs=[pl.BlockSpec(memory_space=VMEM)] * 12,
+        out_specs=[pl.BlockSpec(memory_space=VMEM)] * 3,
         scratch_shapes=[
             VMEM((rows, lanes), jnp.int32),
             VMEM((sites, lanes), F32),
@@ -345,14 +319,35 @@
             VMEM((layers, width, width), BF16),
             VMEM((layers, hidden_width, width), BF16),
             VMEM((layers, width, hidden_width), BF16),
-            VMEM((width, lanes), F32),
+            VMEM((rungs - 1,) + init_up.shape, jnp.int32),
+            VMEM((rungs - 1,) + flip_site.shape, jnp.int32),
+            VMEM((rungs - 1,) + accept.shape, jnp.int32),
+            VMEM((groups - 1,) + accept.shape, jnp.int32),
+            pltpu.SemaphoreType.DMA((rungs - 1, 3)),
+            pltpu.SemaphoreType.DMA((rungs - 1, 3)),
+            pltpu.SemaphoreType.DMA((groups - 1,)),
+            pltpu.SemaphoreType.DMA((groups - 1,)),
         ],
+        compiler_params=pltpu.CompilerParams(collective_id=0, has_side_effects=True),
         name="window",
     )(
-        init_up, flip_site, accept, ups, flips, accepts, counts, swap_ok, ladder_bit.T, w_embed,
+        init_up, flip_site, accept, swap_ok, ladder_bit.T, w_embed,
         pos_embed, w_value, mixing.transpose(1, 2, 0, 3).reshape(-1, patch_count), w_out, w_in,
-        w_back.swapaxes(1, 2), w_final, b_final.reshape(1, width),
-    )
+        w_back.swapaxes(1, 2),
+    )
+    half_side = math.isqrt(sites) // 2
+    proposals, spins, amp, totals = pl.pallas_call(
+        functools.partial(head_kernel, half_side),
+        out_shape=(
+            jax.ShapeDtypeStruct((steps, chains), F32),
+            jax.ShapeDtypeStruct((chains, sites), F32),
+            jax.ShapeDtypeStruct((1, chains), F32),
+            jax.ShapeDtypeStruct((1, steps), F32),
+        ),
+        in_specs=[pl.BlockSpec(memory_space=VMEM)] * 5,
+        out_specs=[pl.BlockSpec(memory_space=VMEM)] * 4,
+        name="head",
+    )(pool, spins, totals, w_final, b_final.reshape(1, width))
     return proposals, spins, amp.reshape(chains), totals
 
 

time: 22.7 us -> 22.5 us (level)
  no operation moved by 1% of the time
where the time goes in v2:
time: 22.5 us; the launch traced here: 22.3 us
  Pallas kernels  21.6 us (96%)
  between operations  0.64 us (3%)
    pallas_call x1, Pallas kernels, on_device(): pl.pallas_call(functools.partial(window_kernel, rungs, groups), out_shape...  19.9 us
    pallas_call x1, Pallas kernels, on_device(): pl.pallas_call(functools.partial(head_kernel, half_side), out_shape=(jax....  1.75 us

profile of v2, /device:TPU:0, one launch (start us, length us, event | category | flops | bytes accessed | tf_op | source)
XLA Modules:
  0.0 22.3 jit_solution(7851938483008924483)
XLA Ops:
  0.6 19.9 %window.1 = (f32[72,128]{1,0:T(8,128)}, f32[16,144]{1,0:T(8,128)}, f32[1,4]{1,0:T(1,128)}) custom-call(s32[16,144]{1,0:T(8,128)} %up_ref.1, s32[4,16]{1,0:T(4,128)} %flip_ref.1, s32[4,16]{1,0:T(4,128)} %accept_ref.1, s32[4,2,16]{2,1,0:T(2,128)} %swap_ref.1, s32[1,4]{1,0:T(1,128)} %bitcast.10, bf16[4,72]{1,0:T(4,128)(2,1)} %w_embed_ref.1, f32[36,72]{1,0:T(8,128)} %pos_ref.1, ...), custom_call_target="tpu_custom_call" | custom-call | tf_op jit(solution)/shard_map/window/pallas_call | solution.py:303
  20.5 1.8 %head.1 = (f32[4,16]{1,0:T(4,128)}, f32[16,144]{1,0:T(8,128)}, f32[1,16]{1,0:T(1,128)}, f32[1,4]{1,0:T(1,128)}) custom-call(f32[72,128]{1,0:T(8,128)} %get-tuple-element.11.pool_ref, f32[16,144]{1,0:T(8,128)} %get-tuple-element.12.spins_ref, f32[1,4]{1,0:T(1,128)} %get-tuple-element.13.totals_ref, f32[72,72]{1,0:T(8,128)} %w_final_ref.1, f32[1,72]{1,0:T(1,128)} %bitcast.9), custom_call_target="tpu_custom_call" | custom-call | tf_op jit(solution)/shard_map/head/pallas_call | solution.py:339

commit v3 on v2

--- a/solution.py
+++ b/solution.py
@@ -43,11 +43,12 @@
 
 
 def window_kernel(
-    rungs, groups, up_ref, flip_ref, accept_ref, swap_ref, bit_ref, w_embed_ref, pos_ref, w_value_ref, mixing_ref, w_out_ref, w_in_ref,
-    w_back_ref,
+    rungs, groups, up_ref, flip_ref, accept_ref, swap_ref, bit_ref, w_embed_hbm, pos_hbm, w_value_hbm, mixing_hbm, w_out_hbm, w_in_hbm,
+    w_back_hbm,
     pool_ref, spins_out_ref, totals_ref,
     event_ref, spin_ref, x_ref, v_ref, embed_ref, wv_ref, wo_ref, wi_ref, wb_ref,
     ups_ref, flips_ref, accepts_ref, counts_ref, send_sem, recv_sem, group_send, group_recv,
+    w_embed_ref, pos_ref, w_value_ref, mixing_ref, w_out_ref, w_in_ref, w_back_ref, load_sem,
 ):
     chains, sites = up_ref.shape
     steps = flip_ref.shape[0]
@@ -68,6 +69,18 @@
     barrier = pltpu.get_barrier_semaphore()
     for device in over_ladder + over_group:
         pl.semaphore_signal(barrier, inc=1, device_id=device, device_id_type=MESH)
+    loads = [
+        pltpu.make_async_copy(source, landing, load_sem.at[index])
+        for index, (source, landing) in enumerate(
+            (
+                (w_embed_hbm, w_embed_ref), (pos_hbm, pos_ref), (w_value_hbm, w_value_ref),
+                (w_out_hbm, w_out_ref), (w_in_hbm, w_in_ref), (w_back_hbm, w_back_ref),
+                (mixing_hbm, mixing_ref),
+            )
+        )
+    ]
+    for load in loads:
+        load.start()
     pl.semaphore_wait(barrier, rungs - 1 + groups - 1)
     walkers = [
         pltpu.make_async_remote_copy(
@@ -96,6 +109,9 @@
     ]
     for copy in walkers + tallies:
         copy.start()
+
+    for load in loads:
+        load.wait()
 
     depth = embed_ref.shape[1]
     part_rows = (depth - 8) // 3
@@ -238,7 +254,7 @@
             streams = [old + matmul(wo_ref[layer], mix) for old, mix in zip(olds, mixes)]
             norms = [layer_norm(stream).astype(BF16) for stream in streams]
             hiddens = [
-                twice_gelu(matmul(wi_ref[layer], norm)).astype(BF16) for norm in norms
+                twice_gelu(matmul(wi_ref[layer], norm).astype(BF16)) for norm in norms
             ]
             streams = [
                 stream + matmul(wb_ref[layer], hidden)
@@ -300,6 +316,11 @@
     lanes = -(-(steps + 1) * chains // 128) * 128
     rows = -(-(steps + 1) // 8) * 8
     depth = 8 + 3 * (-(-patch_count // 8) * 8)
+    weights = (
+        w_embed, pos_embed, w_value,
+        mixing.transpose(1, 2, 0, 3).reshape(-1, patch_count), w_out, w_in,
+        w_back.swapaxes(1, 2),
+    )
     pool, spins, totals = pl.pallas_call(
         functools.partial(window_kernel, rungs, groups),
         out_shape=(
@@ -307,7 +328,8 @@
             jax.ShapeDtypeStruct((chains, sites), F32),
             jax.ShapeDtypeStruct((1, steps), F32),
         ),
-        in_specs=[pl.BlockSpec(memory_space=VMEM)] * 12,
+        in_specs=[pl.BlockSpec(memory_space=VMEM)] * 5
+        + [pl.BlockSpec(memory_space=pl.ANY)] * len(weights),
         out_specs=[pl.BlockSpec(memory_space=VMEM)] * 3,
         scratch_shapes=[
             VMEM((rows, lanes), jnp.int32),
@@ -327,13 +349,13 @@
             pltpu.SemaphoreType.DMA((rungs - 1, 3)),
             pltpu.SemaphoreType.DMA((groups - 1,)),
             pltpu.SemaphoreType.DMA((groups - 1,)),
-        ],
+        ]
+        + [VMEM(weight.shape, weight.dtype) for weight in weights]
+        + [pltpu.SemaphoreType.DMA((len(weights),))],
         compiler_params=pltpu.CompilerParams(collective_id=0, has_side_effects=True),
         name="window",
     )(
-        init_up, flip_site, accept, swap_ok, ladder_bit.T, w_embed,
-        pos_embed, w_value, mixing.transpose(1, 2, 0, 3).reshape(-1, patch_count), w_out, w_in,
-        w_back.swapaxes(1, 2),
+        init_up, flip_site, accept, swap_ok, ladder_bit.T, *weights
     )
     half_side = math.isqrt(sites) // 2
     proposals, spins, amp, totals = pl.pallas_call(

time: 22.5 us -> 20.9 us (0.929)
  Pallas kernels: 21.6 us -> 20 us
    pallas_call x1, Pallas kernels: 19.9 us -> 18.3 us  [on_device(): pl.pallas_call(functools.partial(window_kernel, rungs, groups), out_shape...]
where the time goes in v3:
time: 20.9 us; the launch traced here: 20.6 us
  Pallas kernels  20 us (96%)
  between operations  0.64 us (3%)
    pallas_call x1, Pallas kernels, on_device(): pl.pallas_call(functools.partial(window_kernel, rungs, groups), out_shape...  18.3 us
    pallas_call x1, Pallas kernels, on_device(): pl.pallas_call(functools.partial(head_kernel, half_side), out_shape=(jax....  1.75 us

profile of v3, /device:TPU:0, one launch (start us, length us, event | category | flops | bytes accessed | tf_op | source)
XLA Modules:
  0.0 20.6 jit_solution(18106177411463750751)
XLA Ops:
  0.6 18.3 %window.1 = (f32[72,128]{1,0:T(8,128)}, f32[16,144]{1,0:T(8,128)}, f32[1,4]{1,0:T(1,128)}) custom-call(s32[16,144]{1,0:T(8,128)} %up_ref.1, s32[4,16]{1,0:T(4,128)} %flip_ref.1, s32[4,16]{1,0:T(4,128)} %accept_ref.1, s32[4,2,16]{2,1,0:T(2,128)} %swap_ref.1, s32[1,4]{1,0:T(1,128)} %bitcast.10, bf16[4,72]{1,0:T(4,128)(2,1)} %w_embed_hbm.1, f32[36,72]{1,0:T(8,128)} %pos_hbm.1, ...), custom_call_target="tpu_custom_call" | custom-call | tf_op jit(solution)/shard_map/window/pallas_call | solution.py:324
  18.9 1.8 %head.1 = (f32[4,16]{1,0:T(4,128)}, f32[16,144]{1,0:T(8,128)}, f32[1,16]{1,0:T(1,128)}, f32[1,4]{1,0:T(1,128)}) custom-call(f32[72,128]{1,0:T(8,128)} %get-tuple-element.11.pool_ref, f32[16,144]{1,0:T(8,128)} %get-tuple-element.12.spins_ref, f32[1,4]{1,0:T(1,128)} %get-tuple-element.13.totals_ref, f32[72,72]{1,0:T(8,128)} %w_final_ref.1, f32[1,72]{1,0:T(1,128)} %bitcast.9), custom_call_target="tpu_custom_call" | custom-call | tf_op jit(solution)/shard_map/head/pallas_call | solution.py:361

commit v4 on v3

--- a/solution.py
+++ b/solution.py
@@ -55,7 +55,7 @@
     bits = rungs.bit_length() - 1
     patch_count, width = pos_ref.shape
     layers = w_value_ref.shape[0]
-    heads = mixing_ref.shape[0] // (layers * patch_count)
+    heads = mixing_hbm.shape[0] // (layers * patch_count)
     per_head = width // heads
     hidden_width = w_in_ref.shape[2]
     lanes = event_ref.shape[1]
@@ -75,7 +75,7 @@
             (
                 (w_embed_hbm, w_embed_ref), (pos_hbm, pos_ref), (w_value_hbm, w_value_ref),
                 (w_out_hbm, w_out_ref), (w_in_hbm, w_in_ref), (w_back_hbm, w_back_ref),
-                (mixing_hbm, mixing_ref),
+                (mixing_hbm, mixing_ref.at[pl.ds(0, mixing_hbm.shape[0])]),
             )
         )
     ]
@@ -335,7 +335,7 @@
             VMEM((rows, lanes), jnp.int32),
             VMEM((sites, lanes), F32),
             VMEM((patch_count * width, lanes), F32),
-            VMEM((patch_count * width, lanes), F32),
+            VMEM((-(-patch_count // 8) * 8 * width, lanes), F32),
             VMEM((width, depth), BF16),
             VMEM((layers, width, width), BF16),
             VMEM((layers, width, width), BF16),
@@ -350,7 +350,9 @@
             pltpu.SemaphoreType.DMA((groups - 1,)),
             pltpu.SemaphoreType.DMA((groups - 1,)),
         ]
-        + [VMEM(weight.shape, weight.dtype) for weight in weights]
+        + [VMEM(weight.shape, weight.dtype) for weight in weights[:3]]
+        + [VMEM((weights[3].shape[0] + 8 * layers, patch_count), F32)]
+        + [VMEM(weight.shape, weight.dtype) for weight in weights[4:]]
         + [pltpu.SemaphoreType.DMA((len(weights),))],
         compiler_params=pltpu.CompilerParams(collective_id=0, has_side_effects=True),
         name="window",

time: 20.9 us -> 20.9 us (level)
  no operation moved by 1% of the time
where the time goes in v4:
time: 20.9 us; the launch traced here: 20.7 us
  Pallas kernels  20 us (96%)
  between operations  0.64 us (3%)
    pallas_call x1, Pallas kernels, on_device(): pl.pallas_call(functools.partial(window_kernel, rungs, groups), out_shape...  18.3 us
    pallas_call x1, Pallas kernels, on_device(): pl.pallas_call(functools.partial(head_kernel, half_side), out_shape=(jax....  1.75 us

profile of v4, /device:TPU:0, one launch (start us, length us, event | category | flops | bytes accessed | tf_op | source)
XLA Modules:
  0.0 20.7 jit_solution(7683123265351780272)
XLA Ops:
  0.6 18.3 %window.1 = (f32[72,128]{1,0:T(8,128)}, f32[16,144]{1,0:T(8,128)}, f32[1,4]{1,0:T(1,128)}) custom-call(s32[16,144]{1,0:T(8,128)} %up_ref.1, s32[4,16]{1,0:T(4,128)} %flip_ref.1, s32[4,16]{1,0:T(4,128)} %accept_ref.1, s32[4,2,16]{2,1,0:T(2,128)} %swap_ref.1, s32[1,4]{1,0:T(1,128)} %bitcast.10, bf16[4,72]{1,0:T(4,128)(2,1)} %w_embed_hbm.1, f32[36,72]{1,0:T(8,128)} %pos_hbm.1, ...), custom_call_target="tpu_custom_call" | custom-call | tf_op jit(solution)/shard_map/window/pallas_call | solution.py:324
  18.9 1.8 %head.1 = (f32[4,16]{1,0:T(4,128)}, f32[16,144]{1,0:T(8,128)}, f32[1,16]{1,0:T(1,128)}, f32[1,4]{1,0:T(1,128)}) custom-call(f32[72,128]{1,0:T(8,128)} %get-tuple-element.11.pool_ref, f32[16,144]{1,0:T(8,128)} %get-tuple-element.12.spins_ref, f32[1,4]{1,0:T(1,128)} %get-tuple-element.13.totals_ref, f32[72,72]{1,0:T(8,128)} %w_final_ref.1, f32[1,72]{1,0:T(1,128)} %bitcast.9), custom_call_target="tpu_custom_call" | custom-call | tf_op jit(solution)/shard_map/head/pallas_call | solution.py:363
